TPU v7x, 32 devices: a whole 2x2x4 slice. The times are simulated.
32 devices in a mesh: groups: 2 (over y), expert: 8 (over z, core), attn: 2 (over x).
Axes of the slice: x: 2, y: 2, z: 4, core: 2. Of those that a mesh axis runs over, the one named last changes fastest.
Arguments:
- tokens: bfloat16 [512, 3584], P(('groups', 'expert')), parts along dimension 0, may hold values from -6 to 6
- gates: float32 [512, 8], P(('groups', 'expert')), parts along dimension 0, may hold values from 0.05 to 0.6
- slots: int32 [512, 8], P(('groups', 'expert')), parts along dimension 0, may hold values from 0 to 15, all different within a row; in each aligned block of 32 rows (0 to 31, 32 to 63, ...) at most 20 rows name the same one
- plan: int32 [16], P('groups'), parts along dimension 0, may hold values from 0 to 7, as said below
- gate_proj: bfloat16 [8, 3584, 1024], P('expert', None, 'attn'), may hold values from -0.09375 to 0.09375
- up_proj: bfloat16 [8, 3584, 1024], P('expert', None, 'attn'), may hold values from -0.09375 to 0.09375
- down_proj: bfloat16 [8, 3584, 1024], P('expert', None, 'attn'), may hold values from -0.1875 to 0.1875
Outputs:
- moe_out: bfloat16 [512, 3584], P(('groups', 'expert')), parts along dimension 0
There are 2 independent parts, one for each index of `groups`. A program takes and returns all parts, laid end to end along the dimension named above; an argument that names none is the same for every part. Nothing has to cross between parts.
Inputs may be any that keep to these rules, and one draw needn't show every extreme that they name: A row's 8 slots are distinct; among the 32 rows of one index of expert (aligned blocks) no slot is named more than 20 times, a bound that some block reaches. plan[d] is never d; no expert is named by more than 2 entries of plan, and some expert by exactly 2.
All inputs are finite; a program needn't handle non-finite values.
Results may differ from a plain program's by a relative error of at most 0.014.
Values may be sent and summed in bfloat16 or wider, within the bound.
No kernel may reach another device: no remote copies, remote signals or barrier semaphores. Data moves between devices by JAX's collectives and lax.ppermute only.
A program may use at most 128 MiB of HBM per device.

v0:
```python
import jax
import jax.numpy as jnp
from jax import lax
from jax.sharding import PartitionSpec as P

MULT = 2


def expert_rows(rows, w_gate, w_up, w_down):
    gate_act = jnp.dot(rows, w_gate, preferred_element_type=jnp.float32)
    up_act = jnp.dot(rows, w_up, preferred_element_type=jnp.float32)
    hidden = (jax.nn.silu(gate_act) * up_act).astype(jnp.bfloat16)
    down_out = jnp.einsum("rf,df->rd", hidden, w_down, preferred_element_type=jnp.float32)
    return down_out.astype(jnp.bfloat16)


def slot_ranks(slot_keys, key_count):
    onehot = (slot_keys[:, None] == jnp.arange(key_count, dtype=jnp.int32)[None, :]).astype(
        jnp.int32
    )
    return jnp.sum(jnp.cumsum(onehot, axis=0) * onehot, axis=1) - 1


def spread_rows(row_index, row_total, tok_count, top_count):
    matches = (
        row_index.reshape(tok_count, top_count)[None, :, :]
        == jnp.arange(row_total, dtype=jnp.int32)[:, None, None]
    )
    return jnp.sum(matches.astype(jnp.int32), axis=2).astype(jnp.bfloat16)


def body(tokens, gates, slots, plan, gate_proj, up_proj, down_proj):
    experts = lax.axis_size("expert")
    tok_count, model_width = tokens.shape
    top_count = slots.shape[1]
    capacity = max(2, min(tok_count, tok_count * top_count * 5 // (8 * experts)))
    flat_slots = slots.reshape(-1)
    device = flat_slots // 2
    slot_kind = flat_slots % 2
    owner_device = jnp.where(slot_kind == 0, device, plan[device])
    per_owner = (1 + MULT) * capacity
    position = slot_ranks(owner_device, experts)
    row_index = owner_device * per_owner + position
    row_total = experts * per_owner
    dispatch = spread_rows(row_index, row_total, tok_count, top_count)
    outgoing = jnp.dot(dispatch, tokens, preferred_element_type=jnp.float32).astype(jnp.bfloat16)
    outgoing = outgoing.reshape(experts, per_owner, model_width)
    incoming = lax.all_to_all(outgoing, "expert", split_axis=0, concat_axis=0, tiled=True)
    results = expert_rows(
        incoming.reshape(row_total, model_width), gate_proj[0], up_proj[0], down_proj[0]
    )
    results = results.reshape(experts, per_owner, model_width)
    returned = lax.all_to_all(results, "expert", split_axis=0, concat_axis=0, tiled=True).reshape(
        row_total, model_width
    )
    choice_rows = row_index.reshape(tok_count, top_count)
    partial_value = jnp.zeros((tok_count, returned.shape[1]), jnp.float32)
    for column in range(top_count):
        partial_value = (
            partial_value
            + returned[choice_rows[:, column]].astype(jnp.float32) * gates[:, column][:, None]
        )
    return lax.psum(partial_value.astype(jnp.bfloat16), "attn")


def solution(mesh):
    return jax.shard_map(
        body,
        mesh=mesh,
        in_specs=(
            P(("groups", "expert"), None),
            P(("groups", "expert"), None),
            P(("groups", "expert"), None),
            P("groups"),
            P("expert", None, "attn"),
            P("expert", None, "attn"),
            P("expert", None, "attn"),
        ),
        out_specs=P(("groups", "expert"), None),
        check_vma=False,
    )
```

profile of v0, /device:TPU:0, one launch (start us, length us, event | category | flops | bytes accessed | tf_op | source)
XLA Modules:
  0.0 286.4 jit_solution(9104749936648108147)
XLA Ops:
  6.5 0.8 copy.23
  7.3 0.1 reshape.197
  7.6 1.6 fusion.32
  9.2 4.3 %compare_select_fusion.9 = (s32[256,1]{0,1:T(1,128)S(1)}, s32[256,1]{0,1:T(1,128)S(1)}) fusion(s32[]{:T(128)} %bitcast.1, s32[]{:T(128)} %bitcast.2, s32[]{:T(128)} %bitcast.3, s32[]{:T(128)} %bitcast.4, s32[]{:T(128)} %bitcast.5, s32[]{:T(128)} %bitcast.7, s32[]{:T(128)} %bitcast.6, s32[256,1]{0,1:T(1,128)S(1)} %reshape.197), kind=kLoop, calls=%fused_computation.66 | loop fusion | flops 7680 | bytes 3100 | tf_op jit(solution)/shard_map/gather | solution.py:40
  13.6 0.7 compare_select_fusion.19
  14.3 0.6 reduce-window.6
  14.9 0.2 slice_reduce_fusion
  15.2 0.1 fusion.29
  15.4 0.2 convert_reduce_fusion
  15.7 2.9 convolution_convert_fusion.1
  18.5 4.6 %reshape.201 = bf16[8,60,3584]{2,1,0:T(8,128)(2,1)} reshape(bf16[480,3584]{1,0:T(8,128)(2,1)} %convolution_convert_fusion.1) | data formatting | bytes 6881280 | tf_op jit(solution)/shard_map/reshape | solution.py:47
  23.1 89.2 %all_to_all.10 = bf16[8,60,3584]{2,1,0:T(8,128)(2,1)} all-to-all(bf16[8,60,3584]{2,1,0:T(8,128)(2,1)} %reshape.201), channel_id=1, replica_groups=mesh['groups'=2,'expert'=8,'attn'=2] {'expert'}, dimensions={0} | all-to-all | bytes 6881280 | tf_op jit(solution)/shard_map/all_to_all | solution.py:48
  112.3 4.6 %reshape.202 = bf16[480,3584]{1,0:T(8,128)(2,1)} reshape(bf16[8,60,3584]{2,1,0:T(8,128)(2,1)} %all_to_all.10) | data formatting | bytes 6881280 | tf_op jit(solution)/shard_map/reshape | solution.py:50
  116.9 5.0 %fusion.3 = f32[480,512]{1,0:T(8,128)S(1)} fusion(bf16[480,3584]{1,0:T(8,128)(2,1)} %reshape.202, bf16[1,3584,512]{2,1,0:T(8,128)(2,1)} %param.11), kind=kOutput, calls=%fused_computation.13 | convolution fusion | flops 1761607680 | bytes 8093696 | tf_op jit(solution)/shard_map/dot_general | solution.py:10
  121.9 9.7 %convolution_convert_fusion = bf16[480,3584]{1,0:T(8,128)(2,1)} fusion(bf16[1,3584,512]{2,1,0:T(8,128)(2,1)} %param.13, bf16[480,3584]{1,0:T(8,128)(2,1)} %reshape.202, bf16[1,3584,512]{2,1,0:T(8,128)(2,1)} %param.12, f32[480,512]{1,0:T(8,128)S(1)} %fusion.3), kind=kOutput, calls=%fused_computation.8 | convolution fusion | flops 3526410240 | bytes 15204352 | tf_op jit(solution)/shard_map/rf,df->rd/dot_general | solution.py:13
  131.7 4.6 %reshape.203 = bf16[8,60,3584]{2,1,0:T(8,128)(2,1)} reshape(bf16[480,3584]{1,0:T(8,128)(2,1)} %convolution_convert_fusion) | data formatting | bytes 6881280 | tf_op jit(solution)/shard_map/reshape | solution.py:52
  136.3 4.6 %all-to-all-start.1 = ((bf16[8,60,3584]{2,1,0:T(8,128)(2,1)}), bf16[8,60,3584]{2,1,0:T(8,128)(2,1)}, u32[]{:S(2)}, u32[]{:S(2)}) async-start(bf16[8,60,3584]{2,1,0:T(8,128)(2,1)} %reshape.203), calls=%async_computation.1 | async-start | bytes 7340032 | tf_op jit(solution)/shard_map/all_to_all | solution.py:53
  140.9 0.2 all-reduce.2.cloned.1.call-start
  141.2 0.3 fusion.19
  141.6 82.1 %all-to-all-done.1 = bf16[8,60,3584]{2,1,0:T(8,128)(2,1)} async-done(((bf16[8,60,3584]{2,1,0:T(8,128)(2,1)}), bf16[8,60,3584]{2,1,0:T(8,128)(2,1)}, u32[]{:S(2)}, u32[]{:S(2)}) %all-to-all-start.1) | async-done | bytes 3440672 | tf_op jit(solution)/shard_map/all_to_all | solution.py:53
  223.7 4.6 %reshape.204 = bf16[480,3584]{1,0:T(8,128)(2,1)} reshape(bf16[8,60,3584]{2,1,0:T(8,128)(2,1)} %all-to-all-done.1) | data formatting | bytes 6881280 | tf_op jit(solution)/shard_map/reshape | solution.py:53
  228.3 3.3 %gather_fusion = bf16[32,3584]{1,0:T(8,128)(2,1)S(1)} fusion(bf16[480,3584]{1,0:T(8,128)(2,1)} %reshape.204, s32[1024]{0:T(1024)S(1)} %get-tuple-element.40), kind=kCustom, calls=%fused_computation | custom fusion | bytes 458880 | tf_op jit(solution)/shard_map/gather | solution.py:61
  231.6 3.3 %gather_fusion.1 = bf16[32,3584]{1,0:T(8,128)(2,1)S(1)} fusion(bf16[480,3584]{1,0:T(8,128)(2,1)} %reshape.204, s32[1024]{0:T(1024)S(1)} %get-tuple-element.39), kind=kCustom, calls=%fused_computation.1 | custom fusion | bytes 458880 | tf_op jit(solution)/shard_map/gather | solution.py:61
  234.9 3.3 %gather_fusion.2 = bf16[32,3584]{1,0:T(8,128)(2,1)S(1)} fusion(bf16[480,3584]{1,0:T(8,128)(2,1)} %reshape.204, s32[1024]{0:T(1024)S(1)} %get-tuple-element.38), kind=kCustom, calls=%fused_computation.2 | custom fusion | bytes 458880 | tf_op jit(solution)/shard_map/gather | solution.py:61
  238.3 3.3 %gather_fusion.3 = bf16[32,3584]{1,0:T(8,128)(2,1)S(1)} fusion(bf16[480,3584]{1,0:T(8,128)(2,1)} %reshape.204, s32[1024]{0:T(1024)S(1)} %get-tuple-element.37), kind=kCustom, calls=%fused_computation.3 | custom fusion | bytes 458880 | tf_op jit(solution)/shard_map/gather | solution.py:61
  241.6 3.3 %gather_fusion.4 = bf16[32,3584]{1,0:T(8,128)(2,1)S(1)} fusion(bf16[480,3584]{1,0:T(8,128)(2,1)} %reshape.204, s32[1024]{0:T(1024)S(1)} %get-tuple-element.36), kind=kCustom, calls=%fused_computation.4 | custom fusion | bytes 458880 | tf_op jit(solution)/shard_map/gather | solution.py:61
  244.9 3.3 %gather_fusion.5 = bf16[32,3584]{1,0:T(8,128)(2,1)S(1)} fusion(bf16[480,3584]{1,0:T(8,128)(2,1)} %reshape.204, s32[1024]{0:T(1024)S(1)} %get-tuple-element.35), kind=kCustom, calls=%fused_computation.5 | custom fusion | bytes 458880 | tf_op jit(solution)/shard_map/gather | solution.py:61
  248.2 3.3 %gather_fusion.6 = bf16[32,3584]{1,0:T(8,128)(2,1)S(1)} fusion(bf16[480,3584]{1,0:T(8,128)(2,1)} %reshape.204, s32[1024]{0:T(1024)S(1)} %get-tuple-element.34), kind=kCustom, calls=%fused_computation.6 | custom fusion | bytes 458880 | tf_op jit(solution)/shard_map/gather | solution.py:61
  251.6 3.3 %gather_fusion.7 = bf16[32,3584]{1,0:T(8,128)(2,1)S(1)} fusion(bf16[480,3584]{1,0:T(8,128)(2,1)} %reshape.204, s32[1024]{0:T(1024)S(1)} %get-tuple-element.33), kind=kCustom, calls=%fused_computation.7 | custom fusion | bytes 458880 | tf_op jit(solution)/shard_map/gather | solution.py:61
  254.9 1.1 add_convert_fusion
  256.0 21.9 %all-reduce.2.cloned.1.call-done = bf16[32,3584]{1,0:T(8,128)(2,1)} async-done(((bf16[32,3584]{1,0:T(8,128)(2,1)}), bf16[32,3584]{1,0:T(8,128)(2,1)}) %all-reduce.2.cloned.1.call-update) | async-done | bytes 229392 | tf_op jit(solution)/shard_map/psum | solution.py:63
  277.9 1.6 copy.31
  (21 shorter events, 0.5 us)
Async XLA Ops:
  6.5 9.1 %copy-start = (bf16[32,3584]{1,0:T(8,128)(2,1)S(1)}, bf16[32,3584]{1,0:T(8,128)(2,1)}, u32[]{:S(2)}) copy-start(bf16[32,3584]{1,0:T(8,128)(2,1)} %param.7) | copy-start | bytes 688132
  136.3 5.2 %copy-start.1 = (f32[32,8]{0,1:T(8,128)S(1)}, f32[32,8]{0,1:T(8,128)}, u32[]{:S(2)}) copy-start(f32[32,8]{0,1:T(8,128)} %param.8) | copy-start | bytes 3076
  136.3 87.4 %all-to-all-start.1 = ((bf16[8,60,3584]{2,1,0:T(8,128)(2,1)}), bf16[8,60,3584]{2,1,0:T(8,128)(2,1)}, u32[]{:S(2)}, u32[]{:S(2)}) async-start(bf16[8,60,3584]{2,1,0:T(8,128)(2,1)} %reshape.203), calls=%async_computation.1 | async-start | bytes 7340032 | tf_op jit(solution)/shard_map/all_to_all | solution.py:53
  140.9 137.0 %all-reduce.2.cloned.1.call-start = ((), (), s32[]{:S(2)}) async-start(), calls=%async_computation.2 | async-start | bytes 458752 | tf_op jit(solution)/shard_map/psum | solution.py:63
Sparse Core Ops, SparseCore 0:
  256.2 21.7 all-reduce.1
where the time goes:
time: 287 us; the launch traced here: 286 us
  waiting for transfers between devices  104 us (36%)
  blocking collectives  89.2 us (31%)
  local copies, waits for them, and re-layouts  49.7 us (17%)
  matrix products  17.6 us (6%)
  between operations  13.6 us (5%)
  other arithmetic  7.44 us (3%)
  starting transfers between devices  4.85 us (2%)
    all_to_all x1, blocking collectives, body(): lax.all_to_all(outgoing, 'expert', split_axis=0, concat_axis=0, tiled=True)  89.2 us
    all_to_all x1, waiting for transfers between devices, body(): lax.all_to_all(results, 'expert', split_axis=0, concat_axis=0, tiled=True)  82.1 us
    gather x8, local copies, waits for them, and re-layouts, body(): returned[choice_rows[:, column]].astype(jnp.float32)  26.6 us
    psum x1, waiting for transfers between devices, body(): return lax.psum(partial_value.astype(jnp.bfloat16), 'attn')  21.9 us
    dot_general x1, matrix products, expert_rows(): jnp.einsum('rf,df->rd', hidden, w_down, preferred_element_type=jnp.float32)  9.75 us
  transfers between devices with their start and end apart: 2, of which 2 were waited for; matrix products, arithmetic and copies ran while one was open for 0% of the time, Pallas kernels for 0%

commit v1 on v0

--- a/solution.py
+++ b/solution.py
@@ -4,6 +4,11 @@
 from jax.sharding import PartitionSpec as P
 
 MULT = 2
+
+
+def summed_here(block, mesh_axis):
+    parts = lax.all_gather(block, mesh_axis)
+    return jnp.sum(parts, axis=0)
 
 
 def expert_rows(rows, w_gate, w_up, w_down):
@@ -60,7 +65,7 @@
             partial_value
             + returned[choice_rows[:, column]].astype(jnp.float32) * gates[:, column][:, None]
         )
-    return lax.psum(partial_value.astype(jnp.bfloat16), "attn")
+    return summed_here(partial_value.astype(jnp.bfloat16), "attn")
 
 
 def solution(mesh):

time: 287 us -> 258 us (0.90)
  waiting for transfers between devices: 104 us -> 82.2 us
  between operations: 13.6 us -> 0.19 us
  blocking collectives: 89.2 us -> 96.9 us
    psum x1 -> x0, waiting for transfers between devices: 21.9 us -> none  [body(): return lax.psum(partial_value.astype(jnp.bfloat16), 'attn')]
    all_gather x0 -> x1, blocking collectives: none -> 7.72 us  [summed_here(): parts = lax.all_gather(block, mesh_axis)]
  transfers between devices with their start and end apart: 2 -> 1, of which waited for: 2 -> 1; matrix products, arithmetic and copies ran while one was open for 0% -> 0% of each run, Pallas kernels for 0% -> 0%
where the time goes in v1:
time: 258 us; the launch traced here: 257 us
  blocking collectives  96.9 us (38%)
  waiting for transfers between devices  82.2 us (32%)
  local copies, waits for them, and re-layouts  48 us (19%)
  matrix products  17.6 us (7%)
  other arithmetic  7.56 us (3%)
  starting transfers between devices  4.81 us (2%)
    all_to_all x1, blocking collectives, body(): lax.all_to_all(outgoing, 'expert', split_axis=0, concat_axis=0, tiled=True)  89.2 us
    all_to_all x1, waiting for transfers between devices, body(): lax.all_to_all(results, 'expert', split_axis=0, concat_axis=0, tiled=True)  82.2 us
    gather x8, local copies, waits for them, and re-layouts, body(): returned[choice_rows[:, column]].astype(jnp.float32)  26.6 us
    dot_general x1, matrix products, expert_rows(): jnp.einsum('rf,df->rd', hidden, w_down, preferred_element_type=jnp.float32)  9.75 us
    all_gather x1, blocking collectives, summed_here(): parts = lax.all_gather(block, mesh_axis)  7.72 us
  transfers between devices with their start and end apart: 1, of which 1 were waited for; matrix products, arithmetic and copies ran while one was open for 0% of the time, Pallas kernels for 0%

profile of v1, /device:TPU:0, one launch (start us, length us, event | category | flops | bytes accessed | tf_op | source)
XLA Modules:
  0.0 257.3 jit_solution(2097423692175895989)
XLA Ops:
  0.0 0.8 copy.30
  0.8 0.1 reshape.541
  0.9 0.1 reshape.542
  1.1 1.6 fusion.40
  2.7 4.3 %compare_select_fusion.9 = (s32[256,1]{0,1:T(1,128)S(1)}, s32[256,1]{0,1:T(1,128)S(1)}) fusion(s32[]{:T(128)} %bitcast.1, s32[]{:T(128)} %bitcast.2, s32[]{:T(128)} %bitcast.3, s32[]{:T(128)} %bitcast.4, s32[]{:T(128)} %bitcast.5, s32[]{:T(128)} %bitcast.7, s32[]{:T(128)} %bitcast.6, s32[256,1]{0,1:T(1,128)S(1)} %reshape.541), kind=kLoop, calls=%fused_computation.81 | loop fusion | flops 7680 | bytes 3100 | tf_op jit(solution)/shard_map/gather | solution.py:45
  7.0 0.7 compare_select_fusion.19
  7.8 0.6 reduce-window.6
  8.4 0.2 slice_reduce_fusion
  8.7 0.1 fusion.37
  8.9 0.2 convert_reduce_fusion
  9.1 2.9 %convolution_convert_fusion.1 = bf16[480,3584]{1,0:T(8,128)(2,1)} fusion(bf16[32,3584]{1,0:T(8,128)(2,1)S(1)} %copy-done, s32[480,32]{0,1:T(8,128)S(1)} %convert_reduce_fusion), kind=kOutput, calls=%fused_computation.9 | convolution fusion | flops 111836160 | bytes 3731456 | tf_op jit(solution)/shard_map/dot_general | solution.py:51
  12.0 4.6 %reshape.545 = bf16[8,60,3584]{2,1,0:T(8,128)(2,1)} reshape(bf16[480,3584]{1,0:T(8,128)(2,1)} %convolution_convert_fusion.1) | data formatting | bytes 6881280 | tf_op jit(solution)/shard_map/reshape | solution.py:52
  16.6 89.2 %all_to_all.10 = bf16[8,60,3584]{2,1,0:T(8,128)(2,1)} all-to-all(bf16[8,60,3584]{2,1,0:T(8,128)(2,1)} %reshape.545), channel_id=1, replica_groups=mesh['groups'=2,'expert'=8,'attn'=2] {'expert'}, dimensions={0} | all-to-all | bytes 6881280 | tf_op jit(solution)/shard_map/all_to_all | solution.py:53
  105.8 4.6 %reshape.546 = bf16[480,3584]{1,0:T(8,128)(2,1)} reshape(bf16[8,60,3584]{2,1,0:T(8,128)(2,1)} %all_to_all.10) | data formatting | bytes 6881280 | tf_op jit(solution)/shard_map/reshape | solution.py:55
  110.4 5.0 %fusion.3 = f32[480,512]{1,0:T(8,128)S(1)} fusion(bf16[480,3584]{1,0:T(8,128)(2,1)} %reshape.546, bf16[1,3584,512]{2,1,0:T(8,128)(2,1)} %param.11), kind=kOutput, calls=%fused_computation.13 | convolution fusion | flops 1761607680 | bytes 8093696 | tf_op jit(solution)/shard_map/dot_general | solution.py:15
  115.4 9.7 %convolution_convert_fusion = bf16[480,3584]{1,0:T(8,128)(2,1)} fusion(bf16[1,3584,512]{2,1,0:T(8,128)(2,1)} %param.13, bf16[480,3584]{1,0:T(8,128)(2,1)} %reshape.546, bf16[1,3584,512]{2,1,0:T(8,128)(2,1)} %param.12, f32[480,512]{1,0:T(8,128)S(1)} %fusion.3), kind=kOutput, calls=%fused_computation.8 | convolution fusion | flops 3526410240 | bytes 15204352 | tf_op jit(solution)/shard_map/rf,df->rd/dot_general | solution.py:18
  125.1 4.6 %reshape.547 = bf16[8,60,3584]{2,1,0:T(8,128)(2,1)} reshape(bf16[480,3584]{1,0:T(8,128)(2,1)} %convolution_convert_fusion) | data formatting | bytes 6881280 | tf_op jit(solution)/shard_map/reshape | solution.py:57
  129.8 4.8 %all-to-all-start.1 = ((bf16[8,60,3584]{2,1,0:T(8,128)(2,1)}), bf16[8,60,3584]{2,1,0:T(8,128)(2,1)}, u32[]{:S(2)}, u32[]{:S(2)}) async-start(bf16[8,60,3584]{2,1,0:T(8,128)(2,1)} %reshape.547), calls=%async_computation.1 | async-start | bytes 7340032 | tf_op jit(solution)/shard_map/all_to_all | solution.py:58
  134.6 0.3 fusion.27
  135.0 82.2 %all-to-all-done.1 = bf16[8,60,3584]{2,1,0:T(8,128)(2,1)} async-done(((bf16[8,60,3584]{2,1,0:T(8,128)(2,1)}), bf16[8,60,3584]{2,1,0:T(8,128)(2,1)}, u32[]{:S(2)}, u32[]{:S(2)}) %all-to-all-start.1) | async-done | bytes 3440672 | tf_op jit(solution)/shard_map/all_to_all | solution.py:58
  217.1 4.6 %reshape.548 = bf16[480,3584]{1,0:T(8,128)(2,1)} reshape(bf16[8,60,3584]{2,1,0:T(8,128)(2,1)} %all-to-all-done.1) | data formatting | bytes 6881280 | tf_op jit(solution)/shard_map/reshape | solution.py:58
  221.7 3.3 %gather_fusion = bf16[32,3584]{1,0:T(8,128)(2,1)S(1)} fusion(bf16[480,3584]{1,0:T(8,128)(2,1)} %reshape.548, s32[1024]{0:T(1024)S(1)} %get-tuple-element.40), kind=kCustom, calls=%fused_computation | custom fusion | bytes 458880 | tf_op jit(solution)/shard_map/gather | solution.py:66
  225.1 3.3 %gather_fusion.1 = bf16[32,3584]{1,0:T(8,128)(2,1)S(1)} fusion(bf16[480,3584]{1,0:T(8,128)(2,1)} %reshape.548, s32[1024]{0:T(1024)S(1)} %get-tuple-element.39), kind=kCustom, calls=%fused_computation.1 | custom fusion | bytes 458880 | tf_op jit(solution)/shard_map/gather | solution.py:66
  228.4 3.3 %gather_fusion.2 = bf16[32,3584]{1,0:T(8,128)(2,1)S(1)} fusion(bf16[480,3584]{1,0:T(8,128)(2,1)} %reshape.548, s32[1024]{0:T(1024)S(1)} %get-tuple-element.38), kind=kCustom, calls=%fused_computation.2 | custom fusion | bytes 458880 | tf_op jit(solution)/shard_map/gather | solution.py:66
  231.7 3.3 %gather_fusion.3 = bf16[32,3584]{1,0:T(8,128)(2,1)S(1)} fusion(bf16[480,3584]{1,0:T(8,128)(2,1)} %reshape.548, s32[1024]{0:T(1024)S(1)} %get-tuple-element.37), kind=kCustom, calls=%fused_computation.3 | custom fusion | bytes 458880 | tf_op jit(solution)/shard_map/gather | solution.py:66
  235.0 3.3 %gather_fusion.4 = bf16[32,3584]{1,0:T(8,128)(2,1)S(1)} fusion(bf16[480,3584]{1,0:T(8,128)(2,1)} %reshape.548, s32[1024]{0:T(1024)S(1)} %get-tuple-element.36), kind=kCustom, calls=%fused_computation.4 | custom fusion | bytes 458880 | tf_op jit(solution)/shard_map/gather | solution.py:66
  238.4 3.3 %gather_fusion.5 = bf16[32,3584]{1,0:T(8,128)(2,1)S(1)} fusion(bf16[480,3584]{1,0:T(8,128)(2,1)} %reshape.548, s32[1024]{0:T(1024)S(1)} %get-tuple-element.35), kind=kCustom, calls=%fused_computation.5 | custom fusion | bytes 458880 | tf_op jit(solution)/shard_map/gather | solution.py:66
  241.7 3.3 %gather_fusion.6 = bf16[32,3584]{1,0:T(8,128)(2,1)S(1)} fusion(bf16[480,3584]{1,0:T(8,128)(2,1)} %reshape.548, s32[1024]{0:T(1024)S(1)} %get-tuple-element.34), kind=kCustom, calls=%fused_computation.6 | custom fusion | bytes 458880 | tf_op jit(solution)/shard_map/gather | solution.py:66
  245.0 3.3 %gather_fusion.7 = bf16[32,3584]{1,0:T(8,128)(2,1)S(1)} fusion(bf16[480,3584]{1,0:T(8,128)(2,1)} %reshape.548, s32[1024]{0:T(1024)S(1)} %get-tuple-element.33), kind=kCustom, calls=%fused_computation.7 | custom fusion | bytes 458880 | tf_op jit(solution)/shard_map/gather | solution.py:66
  248.4 0.4 fusion.15
  248.8 7.7 %all_gather.4 = bf16[2,32,3584]{2,1,0:T(8,128)(2,1)S(1)} all-gather(bf16[1,32,3584]{2,1,0:T(8,128)(2,1)S(1)} %fusion.15), channel_id=1, replica_groups=mesh['groups'=2,'expert'=8,'attn'=2] {'attn'}, dimensions={0}, use_global_device_ids=true | all-gather | bytes 688128 | tf_op jit(solution)/shard_map/all_gather | solution.py:10
  256.5 0.8 reduce_sum.32
  (19 shorter events, 0.4 us)
Async XLA Ops:
  0.0 9.1 %copy-start = (bf16[32,3584]{1,0:T(8,128)(2,1)S(1)}, bf16[32,3584]{1,0:T(8,128)(2,1)}, u32[]{:S(2)}) copy-start(bf16[32,3584]{1,0:T(8,128)(2,1)} %param.7) | copy-start | bytes 688132
  129.8 5.2 %copy-start.1 = (f32[32,8]{0,1:T(8,128)S(1)}, f32[32,8]{0,1:T(8,128)}, u32[]{:S(2)}) copy-start(f32[32,8]{0,1:T(8,128)} %param.8) | copy-start | bytes 3076
  129.8 87.4 %all-to-all-start.1 = ((bf16[8,60,3584]{2,1,0:T(8,128)(2,1)}), bf16[8,60,3584]{2,1,0:T(8,128)(2,1)}, u32[]{:S(2)}, u32[]{:S(2)}) async-start(bf16[8,60,3584]{2,1,0:T(8,128)(2,1)} %reshape.547), calls=%async_computation.1 | async-start | bytes 7340032 | tf_op jit(solution)/shard_map/all_to_all | solution.py:58
